TPU v7x, 768 devices: a whole 4x8x12 slice. The times are simulated.
768 devices in a mesh: elem: 32 (over y, x), band: 24 (over z, core).
Axes of the slice: x: 4, y: 8, z: 12, core: 2. Of those that a mesh axis runs over, the one named last changes fastest.
Arguments:
- state: bfloat16 [393216, 256], P(('elem', 'band')), may hold values from -6 to 6
- dest_map: int32 [393216, 1], P(('elem', 'band')), may hold values from 0 to 31; in each aligned block of 512 rows (0 to 511, 512 to 1023, ...) at most 32 rows name the same one
- day_mask: int32 [393216, 1], P(('elem', 'band')), may hold values 0 or 1
- cloud: bfloat16 [786432, 512], P(('elem', 'band')), may hold values from -6 to 6
- conv_in: bfloat16 [768, 256], replicated, may hold values from -0.21875 to 0.21875
- conv_mid: bfloat16 [256, 256], replicated, may hold values from -0.375 to 0.375
- conv_out: bfloat16 [256, 768], replicated, may hold values from -0.375 to 0.375
- rad_in: bfloat16 [768, 256], replicated, may hold values from -0.21875 to 0.21875
- rad_mid: bfloat16 [256, 256], replicated, may hold values from -0.375 to 0.375
- rad_out: bfloat16 [256, 128], replicated, may hold values from -0.375 to 0.375
Outputs:
- tendency: bfloat16 [393216, 256], P(('elem', 'band'))
- new_cloud: bfloat16 [786432, 512], P(('elem', 'band'))
Inputs may be any that keep to these rules, and one draw needn't show every extreme that they name: `dest_map`: among the columns of one device (aligned blocks of 512 rows) no value is named by more than 32 rows, a bound that some block reaches.
All inputs are finite; a program needn't handle non-finite values. No bound on the sum of `day_mask` on one device may be relied on, other than what follows from the above.
Results may differ from a plain program's by a relative error of at most 0.0058.
Values may be sent and summed in bfloat16 or wider, within the bound.
A program may use at most 32 MiB of HBM per device.

v0:
```python
import jax
import jax.numpy as jnp
from jax import lax
from jax.sharding import PartitionSpec as P


def passed_along(block, axis, distance):
    devices = range(lax.axis_size(axis))
    route = [((i - distance) % len(devices), i) for i in devices]
    return lax.ppermute(block, axis, route)


def column_physics(inputs, daylight, cloud, conv_in, conv_mid, conv_out, rad_in, rad_mid, rad_out):
    levels = rad_out.shape[1]
    joined = jnp.concatenate([inputs, cloud], axis=1)
    conv_one = jax.nn.silu(jnp.dot(joined, conv_in, preferred_element_type=jnp.float32)).astype(
        jnp.bfloat16
    )
    conv_two = jax.nn.silu(jnp.dot(conv_one, conv_mid, preferred_element_type=jnp.float32)).astype(
        jnp.bfloat16
    )
    conv_result = jnp.dot(conv_two, conv_out, preferred_element_type=jnp.float32)
    rad_one = jax.nn.silu(jnp.dot(joined, rad_in, preferred_element_type=jnp.float32)).astype(
        jnp.bfloat16
    )
    rad_two = jax.nn.silu(jnp.dot(rad_one, rad_mid, preferred_element_type=jnp.float32)).astype(
        jnp.bfloat16
    )
    rad_result = jnp.dot(rad_two, rad_out, preferred_element_type=jnp.float32)
    heating = daylight.astype(jnp.float32)[:, None] * rad_result
    padded = jnp.concatenate([heating, jnp.zeros_like(heating)], axis=1)
    tendency_rows = (conv_result[:, : 2 * levels] + padded).astype(jnp.bfloat16)
    updated = (cloud.astype(jnp.float32) + conv_result[:, 2 * levels :]).astype(jnp.bfloat16)
    return (tendency_rows, updated)


def slot_places(target, groups, capacity):
    onehot = (target[:, None] == jnp.arange(groups, dtype=jnp.int32)[None, :]).astype(jnp.int32)
    order_in = jnp.sum((jnp.cumsum(onehot, axis=0) - onehot) * onehot, axis=1)
    return target * capacity + order_in


def per_device(
    state, dest_map, day_mask, cloud, conv_in, conv_mid, conv_out, rad_in, rad_mid, rad_out
):
    groups = lax.axis_size("elem")
    band_count = lax.axis_size("band")
    capacity = cloud.shape[0] // groups
    features = state.shape[1]
    weights = (conv_in, conv_mid, conv_out, rad_in, rad_mid, rad_out)
    half_rows = groups // 2 * capacity
    partner = band_count // 2
    target = dest_map[:, 0]
    sun_flag = day_mask[:, 0]
    position = slot_places(target, groups, capacity)
    outgoing = jnp.zeros((groups * capacity, features), jnp.bfloat16).at[position].set(state)
    sunlit = (
        jnp.zeros((groups * capacity,), jnp.bfloat16)
        .at[position]
        .set(sun_flag.astype(jnp.bfloat16))
    )
    arrived, arrived_sun = (
        lax.all_to_all(
            outgoing.reshape(groups, capacity, features),
            "elem",
            split_axis=0,
            concat_axis=0,
            tiled=True,
        ),
        lax.all_to_all(
            sunlit.reshape(groups, capacity), "elem", split_axis=0, concat_axis=0, tiled=True
        ),
    )
    arrived = arrived.reshape(groups * capacity, features)
    arrived_sun = arrived_sun.reshape(groups * capacity)
    borrowed = passed_along(cloud[half_rows:], "band", partner)
    serving_cloud = jnp.concatenate([cloud[:half_rows], borrowed], axis=0)
    tendency_rows, updated = column_physics(arrived, arrived_sun, serving_cloud, *weights)
    handed_back = passed_along(updated[half_rows:], "band", partner)
    new_cloud = jnp.concatenate([updated[:half_rows], handed_back], axis=0)
    returned = lax.all_to_all(
        tendency_rows.reshape(groups, capacity, features),
        "elem",
        split_axis=0,
        concat_axis=0,
        tiled=True,
    )
    tendency = returned.reshape(groups * capacity, features)[position]
    return (tendency, new_cloud)


def solution(mesh):
    placed = (
        P(("elem", "band"), None),
        P(("elem", "band"), None),
        P(("elem", "band"), None),
        P(("elem", "band"), None),
        P(),
        P(),
        P(),
        P(),
        P(),
        P(),
    )
    return jax.shard_map(
        per_device,
        mesh=mesh,
        in_specs=placed,
        out_specs=(P(("elem", "band"), None), P(("elem", "band"), None)),
        check_vma=False,
    )
```

profile of v0, /device:TPU:6, one launch (start us, length us, event | category | flops | bytes accessed | tf_op | source)
XLA Modules:
  0.0 142.7 jit_solution(11131222004213189231)
XLA Ops:
  0.6 0.0 copy-start
  0.6 0.0 copy-start.3
  0.7 0.0 copy-start.6
  0.7 0.8 fusion.13
  1.5 1.2 reduce-window.6
  2.6 0.2 slice_reduce_fusion
  2.9 0.8 fusion.12
  3.7 0.7 compare_select_fusion
  4.4 0.7 convert_reduce_fusion.1
  5.1 3.8 %scatter_custom_fusion.1 = bf16[1024]{0:T(1024)(128)(2,1)S(1)} fusion(s32[512]{0:T(512)S(1)} %bitcast.41, bf16[512]{0:T(512)(128)(2,1)S(1)} %convert_reduce_fusion.1, bf16[]{:T(256)} %constant.7.clone.1), kind=kCustom, calls=%fused_computation.35 | custom fusion | bytes 2050 | tf_op jit(solution)/shard_map/scatter | solution.py:60
  8.9 0.7 all_to_all.16
  9.5 13.0 %all-to-all-start.1 = ((bf16[32,1,32]{2,1,0:T(2,128)(2,1)}), bf16[32,1,32]{2,1,0:T(2,128)(2,1)S(1)}, u32[]{:S(2)}, u32[]{:S(2)}) async-start(bf16[32,1,32]{2,1,0:T(2,128)(2,1)} %all_to_all.16), calls=%async_computation.1 | async-start | bytes 32768 | tf_op jit(solution)/shard_map/all_to_all | solution.py:70
  22.5 3.5 %scatter_custom_fusion = bf16[1024,256]{1,0:T(8,128)(2,1)} fusion(s32[512]{0:T(512)S(1)} %bitcast.42, bf16[512,256]{1,0:T(8,128)(2,1)} %param.10, bf16[]{:T(256)} %constant.7.clone.1), kind=kCustom, calls=%fused_computation.20 | custom fusion | bytes 524800 | tf_op jit(solution)/shard_map/scatter | solution.py:56
  26.0 4.5 %all-to-all-done.1 = bf16[32,1,32]{2,1,0:T(2,128)(2,1)S(1)} async-done(((bf16[32,1,32]{2,1,0:T(2,128)(2,1)}), bf16[32,1,32]{2,1,0:T(2,128)(2,1)S(1)}, u32[]{:S(2)}, u32[]{:S(2)}) %all-to-all-start.1) | async-done | bytes 2080 | tf_op jit(solution)/shard_map/all_to_all | solution.py:70
  30.5 5.6 %all-to-all-start = ((bf16[32,32,256]{2,1,0:T(8,128)(2,1)}), bf16[32,32,256]{2,1,0:T(8,128)(2,1)S(1)}, u32[]{:S(2)}, u32[]{:S(2)}) async-start(bf16[32,32,256]{2,1,0:T(8,128)(2,1)} %bitcast.5), calls=%async_computation | async-start | bytes 1048576 | tf_op jit(solution)/shard_map/all_to_all | solution.py:63
  36.1 0.0 copy-done.3
  36.1 0.1 fusion.23
  36.2 0.0 copy-start.2
  36.2 12.3 %collective-permute-start = (bf16[512,512]{1,0:T(8,128)(2,1)S(1)}, bf16[512,512]{1,0:T(8,128)(2,1)S(1)}, u32[]{:S(2)}, u32[]{:S(2)}) collective-permute-start(bf16[512,512]{1,0:T(8,128)(2,1)S(1)} %get-tuple-element.5), channel_id=1, source_target_pairs={{12,0},{13,1},{14,2},{15,3},{16,4},{17,5},{18,6},{19,7},{20,8},{21... | collective-permute-start | bytes 1572872 | tf_op jit(solution)/shard_map/ppermute | solution.py:10
  48.5 0.1 convert_reduce_fusion
  48.5 0.1 reshape.52
  48.6 11.4 %collective-permute-done = bf16[512,512]{1,0:T(8,128)(2,1)S(1)} collective-permute-done((bf16[512,512]{1,0:T(8,128)(2,1)S(1)}, bf16[512,512]{1,0:T(8,128)(2,1)S(1)}, u32[]{:S(2)}, u32[]{:S(2)}) %collective-permute-start) | collective-permute-done | bytes 524320 | tf_op jit(solution)/shard_map/ppermute | solution.py:10
  60.0 0.0 copy-start.5
  60.0 0.0 all-to-all-done
  60.0 0.0 copy-start.4
  60.0 0.0 copy-done.2
  60.0 0.8 copy-done.5
  60.8 0.2 copy-done.4
  61.0 0.0 copy-done.6
  61.0 2.7 %multiply_convert_fusion.2 = bf16[1024,256]{1,0:T(8,128)(2,1)} fusion(bf16[256,256]{1,0:T(8,128)(2,1)} %param.15, bf16[768,256]{1,0:T(8,128)(2,1)S(1)} %copy-done.6, bf16[512,512]{1,0:T(8,128)(2,1)S(1)} %collective-permute-done, bf16[512,512]{1,0:T(8,128)(2,1)S(1)} %get-tuple-element.4, bf16[1024,256]{1,0:T(8,128)(2,1)S(1)} %bitcast.37), kind=kOutput, calls=%fused_computation.12 | convolution fusion | flops 544210944 | bytes 2621440 | tf_op jit(solution)/shard_map/dot_general | solution.py:19
  63.7 0.0 copy-done
  63.7 1.6 %fusion.24 = f32[1024,768]{1,0:T(8,128)S(1)} fusion(bf16[1024,256]{1,0:T(8,128)(2,1)} %multiply_convert_fusion.2, bf16[256,768]{1,0:T(8,128)(2,1)S(1)} %copy-done), kind=kOutput, calls=%fused_computation.43 | convolution fusion | flops 402653184 | bytes 4063232 | tf_op jit(solution)/shard_map/dot_general | solution.py:22
  65.3 0.0 copy-start.1
  65.3 4.4 %multiply_convert_fusion = bf16[1024,256]{1,0:T(8,128)(2,1)} fusion(bf16[256,256]{1,0:T(8,128)(2,1)} %param.18, bf16[768,256]{1,0:T(8,128)(2,1)} %param.17, bf16[512,512]{1,0:T(8,128)(2,1)} %copy-done.5, bf16[512,512]{1,0:T(8,128)(2,1)} %copy-done.2, bf16[1024,256]{1,0:T(8,128)(2,1)} %bitcast.38), kind=kOutput, calls=%fused_computation.10 | convolution fusion | flops 544210944 | bytes 2621440 | tf_op jit(solution)/shard_map/dot_general | solution.py:26
  69.7 1.3 convolution_multiply_fusion
  71.1 0.0 copy-done.1
  71.1 0.9 fusion.1
  72.0 9.8 %all-to-all-start.2 = ((bf16[32,32,256]{2,1,0:T(8,128)(2,1)}), bf16[32,32,256]{2,1,0:T(8,128)(2,1)S(1)}, u32[]{:S(2)}, u32[]{:S(2)}) async-start(bf16[32,32,256]{2,1,0:T(8,128)(2,1)} %bitcast.36), calls=%async_computation.2 | async-start | bytes 1048576 | tf_op jit(solution)/shard_map/all_to_all | solution.py:81
  81.8 2.2 %fusion = bf16[1024,512]{1,0:T(8,128)(2,1)S(1)} fusion(f32[1024,768]{1,0:T(8,128)} %copy-done.1, bf16[512,512]{1,0:T(8,128)(2,1)} %copy-done.5, bf16[512,512]{1,0:T(8,128)(2,1)} %copy-done.2), kind=kLoop, calls=%fused_computation.4 | loop fusion | flops 3145728 | bytes 4194304 | tf_op jit(solution)/shard_map/convert_element_type | solution.py:33
  83.9 0.1 fusion.22
  84.0 30.9 %collective-permute-start.1 = (bf16[512,512]{1,0:T(8,128)(2,1)S(1)}, bf16[512,512]{1,0:T(8,128)(2,1)S(1)}, u32[]{:S(2)}, u32[]{:S(2)}) collective-permute-start(bf16[512,512]{1,0:T(8,128)(2,1)S(1)} %get-tuple-element.3), channel_id=1, source_target_pairs={{12,0},{13,1},{14,2},{15,3},{16,4},{17,5},{18,6},{19,7},{20,8},{21... | collective-permute-start | bytes 1572872 | tf_op jit(solution)/shard_map/ppermute | solution.py:10
  115.0 24.1 %collective-permute-done.1 = bf16[512,512]{1,0:T(8,128)(2,1)S(1)} collective-permute-done((bf16[512,512]{1,0:T(8,128)(2,1)S(1)}, bf16[512,512]{1,0:T(8,128)(2,1)S(1)}, u32[]{:S(2)}, u32[]{:S(2)}) %collective-permute-start.1) | collective-permute-done | bytes 524320 | tf_op jit(solution)/shard_map/ppermute | solution.py:10
  139.1 1.0 pad_maximum_fusion
  140.1 0.0 all-to-all-done.2
  140.1 2.6 %gather_fusion = bf16[512,256]{1,0:T(8,128)(2,1)} fusion(bf16[1024,256]{1,0:T(8,128)(2,1)S(1)} %bitcast.35, s32[1024]{0:T(1024)S(1)} %pad_clamp_fusion), kind=kCustom, calls=%fused_computation | custom fusion | bytes 526336 | tf_op jit(solution)/shard_map/gather | solution.py:88
  (3 shorter events, 0.0 us)
Async XLA Ops:
  0.6 63.1 %copy-start = (bf16[256,768]{1,0:T(8,128)(2,1)S(1)}, bf16[256,768]{1,0:T(8,128)(2,1)}, u32[]{:S(2)}) copy-start(bf16[256,768]{1,0:T(8,128)(2,1)} %param.16) | copy-start | bytes 1179652
  0.6 35.5 %copy-start.3 = (bf16[1024,512]{1,0:T(8,128)(2,1)S(1)}, bf16[1024,512]{1,0:T(8,128)(2,1)}, u32[]{:S(2)}) copy-start(bf16[1024,512]{1,0:T(8,128)(2,1)} %param.13) | copy-start | bytes 3145732
  0.7 60.3 %copy-start.6 = (bf16[768,256]{1,0:T(8,128)(2,1)S(1)}, bf16[768,256]{1,0:T(8,128)(2,1)}, u32[]{:S(2)}) copy-start(bf16[768,256]{1,0:T(8,128)(2,1)} %param.14) | copy-start | bytes 1179652
  9.5 21.0 %all-to-all-start.1 = ((bf16[32,1,32]{2,1,0:T(2,128)(2,1)}), bf16[32,1,32]{2,1,0:T(2,128)(2,1)S(1)}, u32[]{:S(2)}, u32[]{:S(2)}) async-start(bf16[32,1,32]{2,1,0:T(2,128)(2,1)} %all_to_all.16), calls=%async_computation.1 | async-start | bytes 32768 | tf_op jit(solution)/shard_map/all_to_all | solution.py:70
  30.5 29.5 %all-to-all-start = ((bf16[32,32,256]{2,1,0:T(8,128)(2,1)}), bf16[32,32,256]{2,1,0:T(8,128)(2,1)S(1)}, u32[]{:S(2)}, u32[]{:S(2)}) async-start(bf16[32,32,256]{2,1,0:T(8,128)(2,1)} %bitcast.5), calls=%async_computation | async-start | bytes 1048576 | tf_op jit(solution)/shard_map/all_to_all | solution.py:63
  36.2 23.8 %copy-start.2 = (bf16[512,512]{1,0:T(8,128)(2,1)}, bf16[512,512]{1,0:T(8,128)(2,1)S(1)}, u32[]{:S(2)}) copy-start(bf16[512,512]{1,0:T(8,128)(2,1)S(1)} %get-tuple-element.4) | copy-start | bytes 1572868
  36.2 23.8 %collective-permute-start = (bf16[512,512]{1,0:T(8,128)(2,1)S(1)}, bf16[512,512]{1,0:T(8,128)(2,1)S(1)}, u32[]{:S(2)}, u32[]{:S(2)}) collective-permute-start(bf16[512,512]{1,0:T(8,128)(2,1)S(1)} %get-tuple-element.5), channel_id=1, source_target_pairs={{12,0},{13,1},{14,2},{15,3},{16,4},{17,5},{18,6},{19,7},{20,8},{21... | collective-permute-start | bytes 1572872 | tf_op jit(solution)/shard_map/ppermute | solution.py:10
  60.0 0.8 copy-start.5
  60.0 1.0 copy-start.4
  65.3 5.8 %copy-start.1 = (f32[1024,768]{1,0:T(8,128)}, f32[1024,768]{1,0:T(8,128)S(1)}, u32[]{:S(2)}) copy-start(f32[1024,768]{1,0:T(8,128)S(1)} %fusion.24) | copy-start | bytes 9437188
  72.0 68.1 %all-to-all-start.2 = ((bf16[32,32,256]{2,1,0:T(8,128)(2,1)}), bf16[32,32,256]{2,1,0:T(8,128)(2,1)S(1)}, u32[]{:S(2)}, u32[]{:S(2)}) async-start(bf16[32,32,256]{2,1,0:T(8,128)(2,1)} %bitcast.36), calls=%async_computation.2 | async-start | bytes 1048576 | tf_op jit(solution)/shard_map/all_to_all | solution.py:81
  84.0 55.1 %collective-permute-start.1 = (bf16[512,512]{1,0:T(8,128)(2,1)S(1)}, bf16[512,512]{1,0:T(8,128)(2,1)S(1)}, u32[]{:S(2)}, u32[]{:S(2)}) collective-permute-start(bf16[512,512]{1,0:T(8,128)(2,1)S(1)} %get-tuple-element.3), channel_id=1, source_target_pairs={{12,0},{13,1},{14,2},{15,3},{16,4},{17,5},{18,6},{19,7},{20,8},{21... | collective-permute-start | bytes 1572872 | tf_op jit(solution)/shard_map/ppermute | solution.py:10
where the time goes:
time: 143 us
  starting transfers between devices  71.5 us (50%)
  waiting for transfers between devices  40 us (28%)
  local copies, waits for them, and re-layouts  12 us (8%)
  matrix products  10.1 us (7%)
  other arithmetic  8.34 us (6%)
    ppermute x2, starting transfers between devices, passed_along(): return lax.ppermute(block, axis, route)  43.2 us
    ppermute x2, waiting for transfers between devices, passed_along(): return lax.ppermute(block, axis, route)  35.5 us
    all_to_all x1, starting transfers between devices, per_device(): lax.all_to_all(sunlit.reshape(groups, capacity), 'elem', split_axis=0, co...  13 us
    all_to_all x1, starting transfers between devices, per_device(): lax.all_to_all(tendency_rows.reshape(groups, capacity, features), 'elem',...  9.77 us
    all_to_all x1, starting transfers between devices, per_device(): lax.all_to_all(outgoing.reshape(groups, capacity, features), 'elem', spli...  5.58 us
    all_to_all x1, waiting for transfers between devices, per_device(): lax.all_to_all(sunlit.reshape(groups, capacity), 'elem', split_axis=0, co...  4.47 us
    dot_general x1, matrix products, column_physics(): jnp.dot(rad_one, rad_mid, preferred_element_type=jnp.float32)  4.42 us
    scatter x1, local copies, waits for them, and re-layouts, per_device(): sunlit = jnp.zeros((groups * capacity,), jnp.bfloat16).at[position].set(s...  3.77 us
  transfers between devices with their start and end apart: 5, of which 3 were waited for; matrix products, arithmetic and copies ran while one was open for 5% of the time, Pallas kernels for 0%

commit v1 on v0

v1 whole, which is shorter than its diff:
```python
import jax
import jax.numpy as jnp
from jax import lax
from jax.experimental import pallas as pl
from jax.experimental.pallas import tpu as pltpu
from jax.sharding import PartitionSpec as P

MESH = pl.DeviceIdType.MESH
BF = jnp.bfloat16
F32 = jnp.float32

GROUPS, CAP, COLS, FEAT, HID, LEV, CLOUD = 32, 32, 512, 256, 256, 128, 512
HALF = GROUPS // 2
SLOTS = GROUPS * CAP
BANDS = 24
LEG = 6
CHUNK = 4
ROWS = CHUNK * CAP


def dot(a, b):
    return jnp.dot(a, b, preferred_element_type=F32)


def silu(v):
    return (0.5 * v) * (1.0 + jnp.tanh(0.5 * v))


def kernel(
    dest_ref, day_ref, state_hbm, cloud_hbm, cin_hbm, cmid_hbm, cout_hbm, rin_hbm, rmid_hbm, rout_hbm,
    tend_ref, newcloud_hbm,
    state, cloud, cin, cmid, cout, rin, rmid, rout,
    outgoing, sunlit, arrived, arrived_sun, relay, upper, upper_sun,
    results, second, back_relay, back_here, returned, first_part, select, new_cloud,
    load_sem, out_sem,
    plane_recv, sun_recv, leg1_recv, leg2_recv, upsun_recv, back1_recv, back2_recv, final_recv,
    plane_send, sun_send, leg1_send, leg2_send, upsun_send, back1_send, back2_send, final_send,
):
    e = lax.axis_index("elem")
    b = lax.axis_index("band")
    up = lax.rem(b + LEG, BANDS)
    down = lax.rem(b + BANDS - LEG, BANDS)
    partner = lax.rem(b + BANDS // 2, BANDS)

    def toward(k):
        return lax.rem(b + LEG + (BANDS - 2 * LEG) * lax.rem(k, 2), BANDS)

    loads = [
        pltpu.make_async_copy(src, dst, load_sem.at[i])
        for i, (src, dst) in enumerate(
            (
                (state_hbm, state), (cloud_hbm, cloud), (cin_hbm, cin), (rin_hbm, rin),
                (cmid_hbm, cmid), (rmid_hbm, rmid), (cout_hbm, cout), (rout_hbm, rout),
            )
        )
    ]
    for load in loads:
        load.start()

    barrier = pltpu.get_barrier_semaphore()

    def greet(k, carry):
        pl.semaphore_signal(barrier, inc=1, device_id=(lax.rem(e + k, GROUPS), b), device_id_type=MESH)
        return carry

    lax.fori_loop(1, GROUPS, greet, 0)
    for band in (up, down, partner):
        pl.semaphore_signal(barrier, inc=1, device_id=(e, band), device_id_type=MESH)

    target = dest_ref[...]
    named = (lax.broadcasted_iota(jnp.int32, (GROUPS, COLS), 0) == target).astype(F32)
    earlier = (
        lax.broadcasted_iota(jnp.int32, (COLS, COLS), 0) < lax.broadcasted_iota(jnp.int32, (COLS, COLS), 1)
    ).astype(F32).astype(BF)
    counts = dot(named.astype(BF), earlier)
    order = jnp.sum(counts * named, axis=0, keepdims=True)
    position = target * CAP + order.astype(jnp.int32)
    sun_named = (named * day_ref[...].astype(F32)).astype(BF)
    ranked = (lax.broadcasted_iota(jnp.int32, (128, COLS), 0) == order.astype(jnp.int32)).astype(F32).astype(BF)
    sunlit[:, 0, :] = lax.dot_general(sun_named, ranked, (((1,), (1,)), ((), ())), preferred_element_type=F32)

    loads[0].wait()

    def pack(c, carry):
        slot = lax.broadcasted_iota(jnp.int32, (ROWS, COLS), 0) + c * ROWS
        chosen = (slot == position).astype(F32).astype(BF)
        outgoing[pl.ds(c * CHUNK, CHUNK)] = dot(chosen, state[...]).astype(BF).reshape(CHUNK, CAP, FEAT)
        return carry

    lax.fori_loop(0, GROUPS // CHUNK, pack, 0)

    pl.semaphore_wait(barrier, GROUPS - 1 + 3)

    def plane_copy(d):
        return pltpu.make_async_remote_copy(
            src_ref=outgoing.at[d], dst_ref=arrived.at[e], send_sem=plane_send, recv_sem=plane_recv.at[e],
            device_id=(d, b), device_id_type=MESH,
        )

    def sun_copy(d):
        return pltpu.make_async_remote_copy(
            src_ref=sunlit.at[d], dst_ref=arrived_sun.at[e], send_sem=sun_send, recv_sem=sun_recv.at[e // HALF],
            device_id=(d, b), device_id_type=MESH,
        )

    def send_blocks():
        def one(k, carry):
            d = lax.rem(e + k, GROUPS)
            plane_copy(d).start()
            sun_copy(d).start()
            return carry

        pltpu.make_async_copy(outgoing.at[e], arrived.at[e], plane_recv.at[e]).start()
        pltpu.make_async_copy(sunlit.at[e], arrived_sun.at[e], sun_recv.at[e // HALF]).start()
        lax.fori_loop(1, GROUPS, one, 0)

    @pl.when(e >= HALF)
    def _():
        send_blocks()

    for load in loads[1:]:
        load.wait()

    def cloud_part(c, carry):
        rows = pl.ds(pl.multiple_of(c * ROWS, ROWS), ROWS)
        block = cloud[rows, :]
        first_part[rows, :HID] = dot(block, cin[FEAT:, :])
        first_part[rows, HID:] = dot(block, rin[FEAT:, :])
        return carry

    lax.fori_loop(0, GROUPS // CHUNK, cloud_part, 0)

    @pl.when(e < HALF)
    def _():
        send_blocks()

    def arrival(buffer, sem):
        return pltpu.make_async_copy(buffer, buffer, sem)

    def z_copy(src, dst, k, send_sem, recv_sem):
        return pltpu.make_async_remote_copy(
            src_ref=src, dst_ref=dst.at[k], send_sem=send_sem, recv_sem=recv_sem.at[k],
            device_id=(e, toward(k)), device_id_type=MESH,
        )

    def leg1(k, carry):
        arrival(arrived.at[HALF + k], plane_recv.at[HALF + k]).wait()
        z_copy(arrived.at[HALF + k], relay, k, leg1_send, leg1_recv).start()
        return carry

    lax.fori_loop(0, HALF, leg1, 0)
    arrival(arrived_sun.at[pl.ds(HALF, HALF)], sun_recv.at[1]).wait()
    up_sun = pltpu.make_async_remote_copy(
        src_ref=arrived_sun.at[pl.ds(HALF, HALF)], dst_ref=upper_sun, send_sem=upsun_send, recv_sem=upsun_recv,
        device_id=(e, partner), device_id_type=MESH,
    )
    up_sun.start()

    def leg2(k, carry):
        arrival(relay.at[k], leg1_recv.at[k]).wait()
        z_copy(relay.at[k], upper, k, leg2_send, leg2_recv).start()
        return carry

    lax.fori_loop(0, HALF, leg2, 0)

    def physics(c, half, states, suns):
        rows = pl.ds(pl.multiple_of((half * (HALF // CHUNK) + c) * ROWS, ROWS), ROWS)
        x = states[pl.ds(c * CHUNK, CHUNK)].reshape(ROWS, FEAT)
        row = lax.broadcasted_iota(jnp.int32, (ROWS, HALF), 0) // CAP + c * CHUNK
        source = (row == lax.broadcasted_iota(jnp.int32, (ROWS, HALF), 1)).astype(F32).astype(BF)
        spread = dot(source, suns.astype(BF))
        place = lax.rem(lax.broadcasted_iota(jnp.int32, (ROWS, 128), 0), CAP)
        own = place == lax.broadcasted_iota(jnp.int32, (ROWS, 128), 1)
        daylight = jnp.sum(jnp.where(own, spread, 0.0), axis=1, keepdims=True)
        conv_one = silu(first_part[rows, :HID] + dot(x, cin[:FEAT, :])).astype(BF)
        rad_one = silu(first_part[rows, HID:] + dot(x, rin[:FEAT, :])).astype(BF)
        conv_two = silu(dot(conv_one, cmid[...])).astype(BF)
        rad_two = silu(dot(rad_one, rmid[...])).astype(BF)
        second[rows, :] = conv_two
        conv_result = dot(conv_two, cout[:, : 2 * LEV])
        heating = daylight * dot(rad_two, rout[...])
        blocks = pl.ds((half * (HALF // CHUNK) + c) * CHUNK, CHUNK)
        results[blocks, :, :LEV] = (conv_result[:, :LEV] + heating).astype(BF).reshape(CHUNK, CAP, LEV)
        results[blocks, :, LEV:] = conv_result[:, LEV:].astype(BF).reshape(CHUNK, CAP, LEV)

    def final_copy(src, owner):
        return pltpu.make_async_remote_copy(
            src_ref=src, dst_ref=returned.at[e], send_sem=final_send, recv_sem=final_recv.at[e],
            device_id=(owner, b), device_id_type=MESH,
        )

    def hand_back(src, owner):
        @pl.when(owner != e)
        def _():
            final_copy(src, owner).start()

        @pl.when(owner == e)
        def _():
            pltpu.make_async_copy(src, returned.at[e], final_recv.at[e]).start()

    def lower_arrival(k, carry):
        arrival(arrived.at[k], plane_recv.at[k]).wait()
        return carry

    lax.fori_loop(0, HALF, lower_arrival, 0)
    arrival(arrived_sun.at[pl.ds(0, HALF)], sun_recv.at[0]).wait()

    def lower_chunk(c, carry):
        physics(c, 0, arrived, arrived_sun[:HALF, 0, :])

        def one(j, inner):
            owner = c * CHUNK + j
            hand_back(results.at[owner], owner)
            return inner

        lax.fori_loop(0, CHUNK, one, 0)
        return carry

    lax.fori_loop(0, HALF // CHUNK, lower_chunk, 0)

    up_sun.wait_recv()

    def upper_chunk(c, carry):
        def come(j, inner):
            k = c * CHUNK + j
            arrival(upper.at[k], leg2_recv.at[k]).wait()
            return inner

        lax.fori_loop(0, CHUNK, come, 0)
        physics(c, 1, upper, upper_sun[:, 0, :])

        def one(j, inner):
            k = c * CHUNK + j
            z_copy(results.at[HALF + k], back_relay, k, back1_send, back1_recv).start()
            return inner

        lax.fori_loop(0, CHUNK, one, 0)
        return carry

    lax.fori_loop(0, HALF // CHUNK, upper_chunk, 0)

    def back2(k, carry):
        arrival(back_relay.at[k], back1_recv.at[k]).wait()
        z_copy(back_relay.at[k], back_here, k, back2_send, back2_recv).start()
        return carry

    lax.fori_loop(0, HALF, back2, 0)

    def cloud_update(c, carry):
        rows = pl.ds(pl.multiple_of(c * ROWS, ROWS), ROWS)
        change = dot(second[rows, :], cout[:, 2 * LEV :])
        new_cloud[rows, :] = (cloud[rows, :].astype(F32) + change).astype(BF)
        return carry

    lax.fori_loop(0, GROUPS // CHUNK, cloud_update, 0)
    store = pltpu.make_async_copy(new_cloud, newcloud_hbm, out_sem)
    store.start()

    def final(k, carry):
        arrival(back_here.at[k], back2_recv.at[k]).wait()
        hand_back(back_here.at[k], HALF + k)
        return carry

    lax.fori_loop(0, HALF, final, 0)

    def selection(c, carry):
        rows = pl.ds(pl.multiple_of(c * ROWS, ROWS), ROWS)
        column = lax.broadcasted_iota(jnp.int32, (ROWS, COLS), 0) + c * ROWS
        same = column == lax.broadcasted_iota(jnp.int32, (ROWS, COLS), 1)
        place = jnp.sum(jnp.where(same, position.astype(F32), 0.0), axis=1, keepdims=True).astype(jnp.int32)
        select[rows, :] = (
            lax.broadcasted_iota(jnp.int32, (ROWS, SLOTS), 1) == place
        ).astype(F32).astype(BF)
        return carry

    lax.fori_loop(0, COLS // ROWS, selection, 0)

    def final_arrival(k, carry):
        arrival(returned.at[k], final_recv.at[k]).wait()
        return carry

    lax.fori_loop(0, GROUPS, final_arrival, 0)
    everything = returned[...].reshape(SLOTS, FEAT)

    def gather(c, carry):
        rows = pl.ds(pl.multiple_of(c * ROWS, ROWS), ROWS)
        tend_ref[rows, :] = dot(select[rows, :], everything).astype(BF)
        return carry

    lax.fori_loop(0, COLS // ROWS, gather, 0)

    store.wait()
    arrival(outgoing.at[pl.ds(0, GROUPS - 1)], plane_send).wait()
    arrival(sunlit.at[pl.ds(0, GROUPS - 1)], sun_send).wait()
    arrival(relay, leg1_send).wait()
    arrival(relay, leg2_send).wait()
    up_sun.wait_send()
    arrival(relay, back1_send).wait()
    arrival(relay, back2_send).wait()
    arrival(returned.at[pl.ds(0, GROUPS - 1)], final_send).wait()


def per_device(state, dest_map, day_mask, cloud, conv_in, conv_mid, conv_out, rad_in, rad_mid, rad_out):
    vmem = pl.BlockSpec(memory_space=pltpu.VMEM)
    hbm = pl.BlockSpec(memory_space=pl.ANY)
    dma = pltpu.SemaphoreType.DMA
    half = pltpu.VMEM((HALF, CAP, FEAT), BF)
    whole = pltpu.VMEM((GROUPS, CAP, FEAT), BF)
    tendency, new_cloud = pl.pallas_call(
        kernel,
        name="physics_remap",
        out_shape=(
            jax.ShapeDtypeStruct((COLS, FEAT), BF),
            jax.ShapeDtypeStruct((SLOTS, CLOUD), BF),
        ),
        in_specs=[vmem, vmem] + [hbm] * 8,
        out_specs=(vmem, hbm),
        scratch_shapes=[
            pltpu.VMEM((COLS, FEAT), BF),
            pltpu.VMEM((SLOTS, CLOUD), BF),
            pltpu.VMEM((FEAT + CLOUD, HID), BF),
            pltpu.VMEM((HID, HID), BF),
            pltpu.VMEM((HID, 6 * LEV), BF),
            pltpu.VMEM((FEAT + CLOUD, HID), BF),
            pltpu.VMEM((HID, HID), BF),
            pltpu.VMEM((HID, LEV), BF),
            whole,
            pltpu.VMEM((GROUPS, 1, 128), F32),
            whole,
            pltpu.VMEM((GROUPS, 1, 128), F32),
            half,
            half,
            pltpu.VMEM((HALF, 1, 128), F32),
            whole,
            pltpu.VMEM((SLOTS, HID), BF),
            half,
            half,
            whole,
            pltpu.VMEM((SLOTS, 2 * HID), F32),
            pltpu.VMEM((COLS, SLOTS), BF),
            pltpu.VMEM((SLOTS, CLOUD), BF),
            dma((8,)),
            dma,
            dma((GROUPS,)), dma((2,)), dma((HALF,)), dma((HALF,)), dma, dma((HALF,)), dma((HALF,)), dma((GROUPS,)),
            dma, dma, dma, dma, dma, dma, dma, dma,
        ],
        compiler_params=pltpu.CompilerParams(collective_id=0, has_side_effects=True),
    )(
        dest_map.reshape(1, COLS), day_mask.reshape(1, COLS), state, cloud,
        conv_in, conv_mid, conv_out, rad_in, rad_mid, rad_out,
    )
    return tendency, new_cloud


def solution(mesh):
    rows = P(("elem", "band"), None)
    return jax.shard_map(
        per_device,
        mesh=mesh,
        in_specs=(rows, rows, rows, rows, P(), P(), P(), P(), P(), P()),
        out_specs=(rows, rows),
        check_vma=False,
    )
```

time: 143 us -> 86.4 us (0.60)
  the two profiles are of different devices: /device:TPU:6 before, /device:TPU:112 now
where the time goes in v1:
time: 86.4 us; the launch traced here: 86.1 us
  Pallas kernels  81.6 us (94%)
  local copies, waits for them, and re-layouts  3.93 us (5%)
    pallas_call x1, Pallas kernels, per_device(): pl.pallas_call(kernel, name='physics_remap', out_shape=(jax.ShapeDtypeStr...  81.6 us
    unnamed x2, local copies, waits for them, and re-layouts  3.93 us

profile of v1, /device:TPU:112, one launch (start us, length us, event | category | flops | bytes accessed | tf_op | source)
XLA Modules:
  0.0 86.1 jit_solution(5367065601442800393)
XLA Ops:
  0.6 81.6 %physics_remap.1 = (bf16[512,256]{1,0:T(8,128)(2,1)}, bf16[1024,512]{1,0:T(8,128)(2,1)}) custom-call(s32[1,512]{1,0:T(1,128)} %bitcast.2, s32[1,512]{1,0:T(1,128)} %bitcast.3, bf16[512,256]{1,0:T(8,128)(2,1)} %state_hbm.1, bf16[1024,512]{1,0:T(8,128)(2,1)} %cloud_hbm.1, bf16[768,256]{1,0:T(8,128)(2,1)} %cin_hbm.1, bf16[256,256]{1,0:T(8,128)(2,1)} %cmid_hbm.1, ...), custom_call_target="tpu_custom_call" | custom-call | tf_op jit(solution)/shard_map/physics_remap/pallas_call | solution.py:309
  82.2 1.7 %copy.14 = bf16[512,256]{1,0:T(8,128)(2,1)} copy(bf16[512,256]{1,0:T(8,128)(2,1)} %get-tuple-element.4) | data formatting | bytes 524288
  83.9 2.3 %copy.15 = bf16[1024,512]{1,0:T(8,128)(2,1)} copy(bf16[1024,512]{1,0:T(8,128)(2,1)} %get-tuple-element.5) | data formatting | bytes 2097152

commit v2 on v1

--- a/solution.py
+++ b/solution.py
@@ -14,7 +14,9 @@
 SLOTS = GROUPS * CAP
 BANDS = 24
 LEG = 6
+PIECES = 4
 CHUNK = 4
+WIDTH, HEIGHT = 4, 8
 ROWS = CHUNK * CAP
 
 
@@ -28,10 +30,10 @@
 
 def kernel(
     dest_ref, day_ref, state_hbm, cloud_hbm, cin_hbm, cmid_hbm, cout_hbm, rin_hbm, rmid_hbm, rout_hbm,
-    tend_ref, newcloud_hbm,
+    returned, position_ref, newcloud_hbm,
     state, cloud, cin, cmid, cout, rin, rmid, rout,
     outgoing, sunlit, arrived, arrived_sun, relay, upper, upper_sun,
-    results, second, back_relay, back_here, returned, first_part, select, new_cloud,
+    results, second, back_relay, back_here, first_part, new_cloud,
     load_sem, out_sem,
     plane_recv, sun_recv, leg1_recv, leg2_recv, upsun_recv, back1_recv, back2_recv, final_recv,
     plane_send, sun_send, leg1_send, leg2_send, upsun_send, back1_send, back2_send, final_send,
@@ -42,6 +44,14 @@
     down = lax.rem(b + BANDS - LEG, BANDS)
     partner = lax.rem(b + BANDS // 2, BANDS)
 
+    y = e // WIDTH
+    x = lax.rem(e, WIDTH)
+    rising = ((y >= 2) & (y <= 5)).astype(jnp.int32)
+
+    def nth(i):
+        c = i // CHUNK
+        return (c * rising + (HALF // CHUNK - 1 - c) * (1 - rising)) * CHUNK + lax.rem(x + WIDTH - lax.rem(i, CHUNK), WIDTH)
+
     def toward(k):
         return lax.rem(b + LEG + (BANDS - 2 * LEG) * lax.rem(k, 2), BANDS)
 
@@ -75,6 +85,7 @@
     counts = dot(named.astype(BF), earlier)
     order = jnp.sum(counts * named, axis=0, keepdims=True)
     position = target * CAP + order.astype(jnp.int32)
+    position_ref[...] = position
     sun_named = (named * day_ref[...].astype(F32)).astype(BF)
     ranked = (lax.broadcasted_iota(jnp.int32, (128, COLS), 0) == order.astype(jnp.int32)).astype(F32).astype(BF)
     sunlit[:, 0, :] = lax.dot_general(sun_named, ranked, (((1,), (1,)), ((), ())), preferred_element_type=F32)
@@ -105,7 +116,10 @@
 
     def send_blocks():
         def one(k, carry):
-            d = lax.rem(e + k, GROUPS)
+            step = (k // WIDTH + 1) // 2
+            turn = lax.rem(k // WIDTH, 2)
+            row = lax.rem(y + step * turn + (HEIGHT - step) * (1 - turn), HEIGHT)
+            d = row * WIDTH + lax.rem(x + lax.rem(k, WIDTH), WIDTH)
             plane_copy(d).start()
             sun_copy(d).start()
             return carry
@@ -114,9 +128,7 @@
         pltpu.make_async_copy(sunlit.at[e], arrived_sun.at[e], sun_recv.at[e // HALF]).start()
         lax.fori_loop(1, GROUPS, one, 0)
 
-    @pl.when(e >= HALF)
-    def _():
-        send_blocks()
+    send_blocks()
 
     for load in loads[1:]:
         load.wait()
@@ -130,10 +142,6 @@
 
     lax.fori_loop(0, GROUPS // CHUNK, cloud_part, 0)
 
-    @pl.when(e < HALF)
-    def _():
-        send_blocks()
-
     def arrival(buffer, sem):
         return pltpu.make_async_copy(buffer, buffer, sem)
 
@@ -143,25 +151,32 @@
             device_id=(e, toward(k)), device_id_type=MESH,
         )
 
-    def leg1(k, carry):
+    def leg1(i, carry):
+        k = nth(i)
         arrival(arrived.at[HALF + k], plane_recv.at[HALF + k]).wait()
         z_copy(arrived.at[HALF + k], relay, k, leg1_send, leg1_recv).start()
         return carry
 
-    lax.fori_loop(0, HALF, leg1, 0)
-    arrival(arrived_sun.at[pl.ds(HALF, HALF)], sun_recv.at[1]).wait()
+    lax.fori_loop(0, CHUNK, leg1, 0)
     up_sun = pltpu.make_async_remote_copy(
         src_ref=arrived_sun.at[pl.ds(HALF, HALF)], dst_ref=upper_sun, send_sem=upsun_send, recv_sem=upsun_recv,
         device_id=(e, partner), device_id_type=MESH,
     )
-    up_sun.start()
-
-    def leg2(k, carry):
+    def leg2(i, carry):
+        k = nth(i)
         arrival(relay.at[k], leg1_recv.at[k]).wait()
         z_copy(relay.at[k], upper, k, leg2_send, leg2_recv).start()
         return carry
 
-    lax.fori_loop(0, HALF, leg2, 0)
+    def both(i, carry):
+        leg1(CHUNK + i, carry)
+        leg2(i, carry)
+        return carry
+
+    lax.fori_loop(0, HALF - CHUNK, both, 0)
+    arrival(arrived_sun.at[pl.ds(HALF, HALF)], sun_recv.at[1]).wait()
+    up_sun.start()
+    lax.fori_loop(HALF - CHUNK, HALF, leg2, 0)
 
     def physics(c, half, states, suns):
         rows = pl.ds(pl.multiple_of((half * (HALF // CHUNK) + c) * ROWS, ROWS), ROWS)
@@ -220,17 +235,17 @@
 
     up_sun.wait_recv()
 
-    def upper_chunk(c, carry):
+    def upper_chunk(i, carry):
         def come(j, inner):
-            k = c * CHUNK + j
+            k = nth(i * CHUNK + j)
             arrival(upper.at[k], leg2_recv.at[k]).wait()
             return inner
 
         lax.fori_loop(0, CHUNK, come, 0)
-        physics(c, 1, upper, upper_sun[:, 0, :])
+        physics(nth(i * CHUNK) // CHUNK, 1, upper, upper_sun[:, 0, :])
 
         def one(j, inner):
-            k = c * CHUNK + j
+            k = nth(i * CHUNK + j)
             z_copy(results.at[HALF + k], back_relay, k, back1_send, back1_recv).start()
             return inner
 
@@ -239,7 +254,8 @@
 
     lax.fori_loop(0, HALF // CHUNK, upper_chunk, 0)
 
-    def back2(k, carry):
+    def back2(i, carry):
+        k = nth(i)
         arrival(back_relay.at[k], back1_recv.at[k]).wait()
         z_copy(back_relay.at[k], back_here, k, back2_send, back2_recv).start()
         return carry
@@ -256,39 +272,19 @@
     store = pltpu.make_async_copy(new_cloud, newcloud_hbm, out_sem)
     store.start()
 
-    def final(k, carry):
+    def final(i, carry):
+        k = nth(i)
         arrival(back_here.at[k], back2_recv.at[k]).wait()
         hand_back(back_here.at[k], HALF + k)
         return carry
 
     lax.fori_loop(0, HALF, final, 0)
 
-    def selection(c, carry):
-        rows = pl.ds(pl.multiple_of(c * ROWS, ROWS), ROWS)
-        column = lax.broadcasted_iota(jnp.int32, (ROWS, COLS), 0) + c * ROWS
-        same = column == lax.broadcasted_iota(jnp.int32, (ROWS, COLS), 1)
-        place = jnp.sum(jnp.where(same, position.astype(F32), 0.0), axis=1, keepdims=True).astype(jnp.int32)
-        select[rows, :] = (
-            lax.broadcasted_iota(jnp.int32, (ROWS, SLOTS), 1) == place
-        ).astype(F32).astype(BF)
-        return carry
-
-    lax.fori_loop(0, COLS // ROWS, selection, 0)
-
     def final_arrival(k, carry):
         arrival(returned.at[k], final_recv.at[k]).wait()
         return carry
 
     lax.fori_loop(0, GROUPS, final_arrival, 0)
-    everything = returned[...].reshape(SLOTS, FEAT)
-
-    def gather(c, carry):
-        rows = pl.ds(pl.multiple_of(c * ROWS, ROWS), ROWS)
-        tend_ref[rows, :] = dot(select[rows, :], everything).astype(BF)
-        return carry
-
-    lax.fori_loop(0, COLS // ROWS, gather, 0)
-
     store.wait()
     arrival(outgoing.at[pl.ds(0, GROUPS - 1)], plane_send).wait()
     arrival(sunlit.at[pl.ds(0, GROUPS - 1)], sun_send).wait()
@@ -297,7 +293,35 @@
     up_sun.wait_send()
     arrival(relay, back1_send).wait()
     arrival(relay, back2_send).wait()
-    arrival(returned.at[pl.ds(0, GROUPS - 1)], final_send).wait()
+    arrival(outgoing.at[pl.ds(0, GROUPS - 1)], final_send).wait()
+
+
+def finish(position_ref, returned_hbm, cloud_hbm, tend_ref, newcloud_hbm, returned, cloud, in_sem, out_sem, load_sem):
+    load = pltpu.make_async_copy(returned_hbm, returned, load_sem)
+    load.start()
+    pieces = [pl.ds(i * (SLOTS // PIECES), SLOTS // PIECES) for i in range(PIECES)]
+    come = [pltpu.make_async_copy(cloud_hbm.at[p], cloud.at[p], in_sem.at[i]) for i, p in enumerate(pieces)]
+    go = [pltpu.make_async_copy(cloud.at[p], newcloud_hbm.at[p], out_sem.at[i]) for i, p in enumerate(pieces)]
+    for copy in come:
+        copy.start()
+
+    def place(c):
+        column = lax.broadcasted_iota(jnp.int32, (ROWS, COLS), 0) + c * ROWS
+        same = column == lax.broadcasted_iota(jnp.int32, (ROWS, COLS), 1)
+        own = jnp.where(same, position_ref[...].astype(F32), 0.0)
+        return jnp.sum(own, axis=1, keepdims=True).astype(jnp.int32)
+
+    slots = lax.broadcasted_iota(jnp.int32, (ROWS, SLOTS), 1)
+    places = [place(c) for c in range(COLS // ROWS)]
+    for first, second in zip(come, go):
+        first.wait()
+        second.start()
+    load.wait()
+    for c in range(COLS // ROWS):
+        select = (slots == places[c]).astype(F32).astype(BF)
+        tend_ref[pl.ds(c * ROWS, ROWS), :] = dot(select, returned[...].reshape(SLOTS, FEAT)).astype(BF)
+    for copy in go:
+        copy.wait()
 
 
 def per_device(state, dest_map, day_mask, cloud, conv_in, conv_mid, conv_out, rad_in, rad_mid, rad_out):
@@ -306,15 +330,16 @@
     dma = pltpu.SemaphoreType.DMA
     half = pltpu.VMEM((HALF, CAP, FEAT), BF)
     whole = pltpu.VMEM((GROUPS, CAP, FEAT), BF)
-    tendency, new_cloud = pl.pallas_call(
+    returned, position, new_cloud = pl.pallas_call(
         kernel,
         name="physics_remap",
         out_shape=(
-            jax.ShapeDtypeStruct((COLS, FEAT), BF),
+            jax.ShapeDtypeStruct((GROUPS, CAP, FEAT), BF),
+            jax.ShapeDtypeStruct((1, COLS), jnp.int32),
             jax.ShapeDtypeStruct((SLOTS, CLOUD), BF),
         ),
         in_specs=[vmem, vmem] + [hbm] * 8,
-        out_specs=(vmem, hbm),
+        out_specs=(hbm, vmem, hbm),
         scratch_shapes=[
             pltpu.VMEM((COLS, FEAT), BF),
             pltpu.VMEM((SLOTS, CLOUD), BF),
@@ -335,9 +360,7 @@
             pltpu.VMEM((SLOTS, HID), BF),
             half,
             half,
-            whole,
             pltpu.VMEM((SLOTS, 2 * HID), F32),
-            pltpu.VMEM((COLS, SLOTS), BF),
             pltpu.VMEM((SLOTS, CLOUD), BF),
             dma((8,)),
             dma,
@@ -349,7 +372,17 @@
         dest_map.reshape(1, COLS), day_mask.reshape(1, COLS), state, cloud,
         conv_in, conv_mid, conv_out, rad_in, rad_mid, rad_out,
     )
-    return tendency, new_cloud
+    return pl.pallas_call(
+        finish,
+        name="finish",
+        out_shape=(
+            jax.ShapeDtypeStruct((COLS, FEAT), BF),
+            jax.ShapeDtypeStruct((SLOTS, CLOUD), BF),
+        ),
+        in_specs=[vmem, hbm, hbm],
+        out_specs=(vmem, hbm),
+        scratch_shapes=[whole, pltpu.VMEM((SLOTS, CLOUD), BF), dma((PIECES,)), dma((PIECES,)), dma],
+    )(position, returned, new_cloud)
 
 
 def solution(mesh):

time: 86.4 us -> 77.9 us (0.902)
  the two profiles are of different devices: /device:TPU:112 before, /device:TPU:120 now
where the time goes in v2:
time: 77.9 us; the launch traced here: 77.6 us
  Pallas kernels  77 us (99%)
    pallas_call x1, Pallas kernels, per_device(): pl.pallas_call(kernel, name='physics_remap', out_shape=(jax.ShapeDtypeStr...  73.5 us
    pallas_call x1, Pallas kernels, per_device(): pl.pallas_call(finish, name='finish', out_shape=(jax.ShapeDtypeStruct((CO...  3.5 us

profile of v2, /device:TPU:120, one launch (start us, length us, event | category | flops | bytes accessed | tf_op | source)
XLA Modules:
  0.0 77.6 jit_solution(12553070711554269075)
XLA Ops:
  0.6 73.5 %physics_remap.1 = (bf16[32,32,256]{2,1,0:T(8,128)(2,1)}, s32[1,512]{1,0:T(1,128)}, bf16[1024,512]{1,0:T(8,128)(2,1)}) custom-call(s32[1,512]{1,0:T(1,128)} %bitcast.2, s32[1,512]{1,0:T(1,128)} %bitcast.3, bf16[512,256]{1,0:T(8,128)(2,1)} %state_hbm.1, bf16[1024,512]{1,0:T(8,128)(2,1)} %cloud_hbm.1, bf16[768,256]{1,0:T(8,128)(2,1)} %cin_hbm.1, ...), custom_call_target="tpu_custom_call" | custom-call | tf_op jit(solution)/shard_map/physics_remap/pallas_call | solution.py:333
  74.1 3.5 %finish.1 = (bf16[512,256]{1,0:T(8,128)(2,1)}, bf16[1024,512]{1,0:T(8,128)(2,1)}) custom-call(s32[1,512]{1,0:T(1,128)} %get-tuple-element.5.position_ref, bf16[32,32,256]{2,1,0:T(8,128)(2,1)} %get-tuple-element.6.returned_hbm, bf16[1024,512]{1,0:T(8,128)(2,1)} %get-tuple-element.7.cloud_hbm), custom_call_target="tpu_custom_call" | custom-call | tf_op jit(solution)/shard_map/finish/pallas_call | solution.py:375

commit v3 on v2

--- a/solution.py
+++ b/solution.py
@@ -14,7 +14,12 @@
 SLOTS = GROUPS * CAP
 BANDS = 24
 LEG = 6
-PIECES = 4
+ARRIVAL = [
+    sum(place * 4**n for n, place in enumerate(order))
+    for order in (
+        (3, 2, 1, 0), (3, 2, 0, 1), (0, 3, 1, 2), (0, 1, 2, 3), (0, 1, 2, 3), (1, 0, 2, 3), (2, 1, 3, 0), (3, 2, 1, 0),
+    )
+]
 CHUNK = 4
 WIDTH, HEIGHT = 4, 8
 ROWS = CHUNK * CAP
@@ -30,11 +35,11 @@
 
 def kernel(
     dest_ref, day_ref, state_hbm, cloud_hbm, cin_hbm, cmid_hbm, cout_hbm, rin_hbm, rmid_hbm, rout_hbm,
-    returned, position_ref, newcloud_hbm,
+    returned, select, new_cloud,
     state, cloud, cin, cmid, cout, rin, rmid, rout,
     outgoing, sunlit, arrived, arrived_sun, relay, upper, upper_sun,
-    results, second, back_relay, back_here, first_part, new_cloud,
-    load_sem, out_sem,
+    results, second, back_relay, back_here, first_part,
+    load_sem,
     plane_recv, sun_recv, leg1_recv, leg2_recv, upsun_recv, back1_recv, back2_recv, final_recv,
     plane_send, sun_send, leg1_send, leg2_send, upsun_send, back1_send, back2_send, final_send,
 ):
@@ -46,14 +51,25 @@
 
     y = e // WIDTH
     x = lax.rem(e, WIDTH)
-    rising = ((y >= 2) & (y <= 5)).astype(jnp.int32)
+    code = sum((y == row).astype(jnp.int32) * digits for row, digits in enumerate(ARRIVAL))
 
     def nth(i):
-        c = i // CHUNK
-        return (c * rising + (HALF // CHUNK - 1 - c) * (1 - rising)) * CHUNK + lax.rem(x + WIDTH - lax.rem(i, CHUNK), WIDTH)
+        n = i // CHUNK
+        weight = 1 + 3 * (n >= 1).astype(jnp.int32) + 12 * (n >= 2).astype(jnp.int32) + 48 * (n >= 3).astype(jnp.int32)
+        return lax.rem(code // weight, 4) * CHUNK + lax.rem(x + WIDTH - lax.rem(i, CHUNK), WIDTH)
 
     def toward(k):
         return lax.rem(b + LEG + (BANDS - 2 * LEG) * lax.rem(k, 2), BANDS)
+
+    barrier = pltpu.get_barrier_semaphore()
+
+    def greet(k, carry):
+        pl.semaphore_signal(barrier, inc=1, device_id=(lax.rem(e + k, GROUPS), b), device_id_type=MESH)
+        return carry
+
+    for band in (partner, up, down):
+        pl.semaphore_signal(barrier, inc=1, device_id=(e, band), device_id_type=MESH)
+    lax.fori_loop(1, GROUPS, greet, 0)
 
     loads = [
         pltpu.make_async_copy(src, dst, load_sem.at[i])
@@ -66,16 +82,6 @@
     ]
     for load in loads:
         load.start()
-
-    barrier = pltpu.get_barrier_semaphore()
-
-    def greet(k, carry):
-        pl.semaphore_signal(barrier, inc=1, device_id=(lax.rem(e + k, GROUPS), b), device_id_type=MESH)
-        return carry
-
-    lax.fori_loop(1, GROUPS, greet, 0)
-    for band in (up, down, partner):
-        pl.semaphore_signal(barrier, inc=1, device_id=(e, band), device_id_type=MESH)
 
     target = dest_ref[...]
     named = (lax.broadcasted_iota(jnp.int32, (GROUPS, COLS), 0) == target).astype(F32)
@@ -85,7 +91,6 @@
     counts = dot(named.astype(BF), earlier)
     order = jnp.sum(counts * named, axis=0, keepdims=True)
     position = target * CAP + order.astype(jnp.int32)
-    position_ref[...] = position
     sun_named = (named * day_ref[...].astype(F32)).astype(BF)
     ranked = (lax.broadcasted_iota(jnp.int32, (128, COLS), 0) == order.astype(jnp.int32)).astype(F32).astype(BF)
     sunlit[:, 0, :] = lax.dot_general(sun_named, ranked, (((1,), (1,)), ((), ())), preferred_element_type=F32)
@@ -269,8 +274,16 @@
         return carry
 
     lax.fori_loop(0, GROUPS // CHUNK, cloud_update, 0)
-    store = pltpu.make_async_copy(new_cloud, newcloud_hbm, out_sem)
-    store.start()
+
+    def selection(c, carry):
+        rows = pl.ds(pl.multiple_of(c * ROWS, ROWS), ROWS)
+        column = lax.broadcasted_iota(jnp.int32, (ROWS, COLS), 0) + c * ROWS
+        same = column == lax.broadcasted_iota(jnp.int32, (ROWS, COLS), 1)
+        place = jnp.sum(jnp.where(same, position.astype(F32), 0.0), axis=1, keepdims=True).astype(jnp.int32)
+        select[rows, :] = (lax.broadcasted_iota(jnp.int32, (ROWS, SLOTS), 1) == place).astype(F32).astype(BF)
+        return carry
+
+    lax.fori_loop(0, COLS // ROWS, selection, 0)
 
     def final(i, carry):
         k = nth(i)
@@ -285,7 +298,6 @@
         return carry
 
     lax.fori_loop(0, GROUPS, final_arrival, 0)
-    store.wait()
     arrival(outgoing.at[pl.ds(0, GROUPS - 1)], plane_send).wait()
     arrival(sunlit.at[pl.ds(0, GROUPS - 1)], sun_send).wait()
     arrival(relay, leg1_send).wait()
@@ -296,32 +308,18 @@
     arrival(outgoing.at[pl.ds(0, GROUPS - 1)], final_send).wait()
 
 
-def finish(position_ref, returned_hbm, cloud_hbm, tend_ref, newcloud_hbm, returned, cloud, in_sem, out_sem, load_sem):
-    load = pltpu.make_async_copy(returned_hbm, returned, load_sem)
-    load.start()
-    pieces = [pl.ds(i * (SLOTS // PIECES), SLOTS // PIECES) for i in range(PIECES)]
-    come = [pltpu.make_async_copy(cloud_hbm.at[p], cloud.at[p], in_sem.at[i]) for i, p in enumerate(pieces)]
-    go = [pltpu.make_async_copy(cloud.at[p], newcloud_hbm.at[p], out_sem.at[i]) for i, p in enumerate(pieces)]
-    for copy in come:
-        copy.start()
-
-    def place(c):
-        column = lax.broadcasted_iota(jnp.int32, (ROWS, COLS), 0) + c * ROWS
-        same = column == lax.broadcasted_iota(jnp.int32, (ROWS, COLS), 1)
-        own = jnp.where(same, position_ref[...].astype(F32), 0.0)
-        return jnp.sum(own, axis=1, keepdims=True).astype(jnp.int32)
-
-    slots = lax.broadcasted_iota(jnp.int32, (ROWS, SLOTS), 1)
-    places = [place(c) for c in range(COLS // ROWS)]
-    for first, second in zip(come, go):
-        first.wait()
-        second.start()
-    load.wait()
+def finish(select, returned, cloud, tend_hbm, newcloud_hbm, tend, sem, tend_sem):
+    store = pltpu.make_async_copy(cloud, newcloud_hbm, sem)
+    store.start()
+    outs = []
     for c in range(COLS // ROWS):
-        select = (slots == places[c]).astype(F32).astype(BF)
-        tend_ref[pl.ds(c * ROWS, ROWS), :] = dot(select, returned[...].reshape(SLOTS, FEAT)).astype(BF)
-    for copy in go:
-        copy.wait()
+        rows = pl.ds(c * ROWS, ROWS)
+        tend[rows, :] = dot(select[rows, :], returned[...].reshape(SLOTS, FEAT)).astype(BF)
+        outs.append(pltpu.make_async_copy(tend.at[rows], tend_hbm.at[rows], tend_sem.at[c]))
+        outs[-1].start()
+    for out in outs:
+        out.wait()
+    store.wait()
 
 
 def per_device(state, dest_map, day_mask, cloud, conv_in, conv_mid, conv_out, rad_in, rad_mid, rad_out):
@@ -330,16 +328,16 @@
     dma = pltpu.SemaphoreType.DMA
     half = pltpu.VMEM((HALF, CAP, FEAT), BF)
     whole = pltpu.VMEM((GROUPS, CAP, FEAT), BF)
-    returned, position, new_cloud = pl.pallas_call(
+    returned, select, new_cloud = pl.pallas_call(
         kernel,
         name="physics_remap",
         out_shape=(
-            jax.ShapeDtypeStruct((GROUPS, CAP, FEAT), BF),
-            jax.ShapeDtypeStruct((1, COLS), jnp.int32),
-            jax.ShapeDtypeStruct((SLOTS, CLOUD), BF),
+            whole,
+            pltpu.VMEM((COLS, SLOTS), BF),
+            pltpu.VMEM((SLOTS, CLOUD), BF),
         ),
         in_specs=[vmem, vmem] + [hbm] * 8,
-        out_specs=(hbm, vmem, hbm),
+        out_specs=(vmem, vmem, vmem),
         scratch_shapes=[
             pltpu.VMEM((COLS, FEAT), BF),
             pltpu.VMEM((SLOTS, CLOUD), BF),
@@ -361,9 +359,7 @@
             half,
             half,
             pltpu.VMEM((SLOTS, 2 * HID), F32),
-            pltpu.VMEM((SLOTS, CLOUD), BF),
             dma((8,)),
-            dma,
             dma((GROUPS,)), dma((2,)), dma((HALF,)), dma((HALF,)), dma, dma((HALF,)), dma((HALF,)), dma((GROUPS,)),
             dma, dma, dma, dma, dma, dma, dma, dma,
         ],
@@ -379,10 +375,10 @@
             jax.ShapeDtypeStruct((COLS, FEAT), BF),
             jax.ShapeDtypeStruct((SLOTS, CLOUD), BF),
         ),
-        in_specs=[vmem, hbm, hbm],
-        out_specs=(vmem, hbm),
-        scratch_shapes=[whole, pltpu.VMEM((SLOTS, CLOUD), BF), dma((PIECES,)), dma((PIECES,)), dma],
-    )(position, returned, new_cloud)
+        in_specs=[vmem, vmem, vmem],
+        out_specs=(hbm, hbm),
+        scratch_shapes=[pltpu.VMEM((COLS, FEAT), BF), dma, dma((COLS // ROWS,))],
+    )(pltpu.with_memory_space_constraint(select, pltpu.VMEM), pltpu.with_memory_space_constraint(returned, pltpu.VMEM), pltpu.with_memory_space_constraint(new_cloud, pltpu.VMEM))
 
 
 def solution(mesh):

time: 77.9 us -> 75.1 us (0.964)
  the two profiles are of different devices: /device:TPU:120 before, /device:TPU:48 now
where the time goes in v3:
time: 75.1 us; the launch traced here: 75 us
  Pallas kernels  74.3 us (99%)
    pallas_call x1, Pallas kernels, per_device(): pl.pallas_call(kernel, name='physics_remap', out_shape=(whole, pltpu.VMEM...  73.2 us

profile of v3, /device:TPU:48, one launch (start us, length us, event | category | flops | bytes accessed | tf_op | source)
XLA Modules:
  0.0 75.0 jit_solution(4449587338433455115)
XLA Ops:
  0.6 73.2 %physics_remap.1 = (bf16[32,32,256]{2,1,0:T(8,128)(2,1)S(1)}, bf16[512,1024]{1,0:T(8,128)(2,1)S(1)}, bf16[1024,512]{1,0:T(8,128)(2,1)S(1)}) custom-call(s32[1,512]{1,0:T(1,128)} %bitcast.2, s32[1,512]{1,0:T(1,128)} %bitcast.3, bf16[512,256]{1,0:T(8,128)(2,1)} %state_hbm.1, bf16[1024,512]{1,0:T(8,128)(2,1)} %cloud_hbm.1, bf16[768,256]{1,0:T(8,128)(2,1)} %cin_hbm.1, ...), custom_call_target="tpu_custom_call" | custom-call | tf_op jit(solution)/shard_map/physics_remap/pallas_call | solution.py:331
  73.8 1.2 %finish.1 = (bf16[512,256]{1,0:T(8,128)(2,1)}, bf16[1024,512]{1,0:T(8,128)(2,1)}) custom-call(bf16[512,1024]{1,0:T(8,128)(2,1)S(1)} %get-tuple-element.5.select, bf16[32,32,256]{2,1,0:T(8,128)(2,1)S(1)} %get-tuple-element.6.returned, bf16[1024,512]{1,0:T(8,128)(2,1)S(1)} %get-tuple-element.7.cloud), custom_call_target="tpu_custom_call" | custom-call | tf_op jit(solution)/shard_map/finish/pallas_call | solution.py:371

commit v4 on v3

--- a/solution.py
+++ b/solution.py
@@ -20,6 +20,7 @@
         (3, 2, 1, 0), (3, 2, 0, 1), (0, 3, 1, 2), (0, 1, 2, 3), (0, 1, 2, 3), (1, 0, 2, 3), (2, 1, 3, 0), (3, 2, 1, 0),
     )
 ]
+LAG = 1
 CHUNK = 4
 WIDTH, HEIGHT = 4, 8
 ROWS = CHUNK * CAP
@@ -115,7 +116,7 @@
 
     def sun_copy(d):
         return pltpu.make_async_remote_copy(
-            src_ref=sunlit.at[d], dst_ref=arrived_sun.at[e], send_sem=sun_send, recv_sem=sun_recv.at[e // HALF],
+            src_ref=sunlit.at[d], dst_ref=arrived_sun.at[e], send_sem=sun_send, recv_sem=sun_recv.at[e // CHUNK],
             device_id=(d, b), device_id_type=MESH,
         )
 
@@ -130,7 +131,7 @@
             return carry
 
         pltpu.make_async_copy(outgoing.at[e], arrived.at[e], plane_recv.at[e]).start()
-        pltpu.make_async_copy(sunlit.at[e], arrived_sun.at[e], sun_recv.at[e // HALF]).start()
+        pltpu.make_async_copy(sunlit.at[e], arrived_sun.at[e], sun_recv.at[e // CHUNK]).start()
         lax.fori_loop(1, GROUPS, one, 0)
 
     send_blocks()
@@ -162,33 +163,48 @@
         z_copy(arrived.at[HALF + k], relay, k, leg1_send, leg1_recv).start()
         return carry
 
-    lax.fori_loop(0, CHUNK, leg1, 0)
-    up_sun = pltpu.make_async_remote_copy(
-        src_ref=arrived_sun.at[pl.ds(HALF, HALF)], dst_ref=upper_sun, send_sem=upsun_send, recv_sem=upsun_recv,
-        device_id=(e, partner), device_id_type=MESH,
-    )
+    def sun_row(n):
+        return nth(n * CHUNK) // CHUNK
+
+    def up_sun(n):
+        q = sun_row(n)
+        rows = pl.ds(HALF + q * CHUNK, CHUNK)
+        arrival(arrived_sun.at[rows], sun_recv.at[HALF // CHUNK + q]).wait()
+        pltpu.make_async_remote_copy(
+            src_ref=arrived_sun.at[rows], dst_ref=upper_sun.at[pl.ds(q * CHUNK, CHUNK)],
+            send_sem=upsun_send, recv_sem=upsun_recv.at[q], device_id=(e, partner), device_id_type=MESH,
+        ).start()
+
     def leg2(i, carry):
         k = nth(i)
         arrival(relay.at[k], leg1_recv.at[k]).wait()
         z_copy(relay.at[k], upper, k, leg2_send, leg2_recv).start()
         return carry
 
-    def both(i, carry):
-        leg1(CHUNK + i, carry)
-        leg2(i, carry)
-        return carry
-
-    lax.fori_loop(0, HALF - CHUNK, both, 0)
-    arrival(arrived_sun.at[pl.ds(HALF, HALF)], sun_recv.at[1]).wait()
-    up_sun.start()
-    lax.fori_loop(HALF - CHUNK, HALF, leg2, 0)
+    def first_legs(n, carry):
+        lax.fori_loop(n * CHUNK, (n + 1) * CHUNK, leg1, 0)
+        up_sun(n)
+        return carry
+
+    def both_legs(n, carry):
+        def both(i, inner):
+            leg1(i, inner)
+            leg2(i - LAG * CHUNK, inner)
+            return inner
+
+        lax.fori_loop(n * CHUNK, (n + 1) * CHUNK, both, 0)
+        up_sun(n)
+        return carry
+
+    lax.fori_loop(0, LAG, first_legs, 0)
+    lax.fori_loop(LAG, HALF // CHUNK, both_legs, 0)
+    lax.fori_loop(HALF - LAG * CHUNK, HALF, leg2, 0)
 
     def physics(c, half, states, suns):
         rows = pl.ds(pl.multiple_of((half * (HALF // CHUNK) + c) * ROWS, ROWS), ROWS)
         x = states[pl.ds(c * CHUNK, CHUNK)].reshape(ROWS, FEAT)
-        row = lax.broadcasted_iota(jnp.int32, (ROWS, HALF), 0) // CAP + c * CHUNK
-        source = (row == lax.broadcasted_iota(jnp.int32, (ROWS, HALF), 1)).astype(F32).astype(BF)
-        spread = dot(source, suns.astype(BF))
+        flags = suns[pl.ds(c * CHUNK, CHUNK), 0, :]
+        spread = jnp.broadcast_to(flags[:, None, :], (CHUNK, CAP, 128)).reshape(ROWS, 128)
         place = lax.rem(lax.broadcasted_iota(jnp.int32, (ROWS, 128), 0), CAP)
         own = place == lax.broadcasted_iota(jnp.int32, (ROWS, 128), 1)
         daylight = jnp.sum(jnp.where(own, spread, 0.0), axis=1, keepdims=True)
@@ -223,10 +239,15 @@
         return carry
 
     lax.fori_loop(0, HALF, lower_arrival, 0)
-    arrival(arrived_sun.at[pl.ds(0, HALF)], sun_recv.at[0]).wait()
+
+    def lower_sun(q, carry):
+        arrival(arrived_sun.at[pl.ds(q * CHUNK, CHUNK)], sun_recv.at[q]).wait()
+        return carry
+
+    lax.fori_loop(0, HALF // CHUNK, lower_sun, 0)
 
     def lower_chunk(c, carry):
-        physics(c, 0, arrived, arrived_sun[:HALF, 0, :])
+        physics(c, 0, arrived, arrived_sun)
 
         def one(j, inner):
             owner = c * CHUNK + j
@@ -237,8 +258,6 @@
         return carry
 
     lax.fori_loop(0, HALF // CHUNK, lower_chunk, 0)
-
-    up_sun.wait_recv()
 
     def upper_chunk(i, carry):
         def come(j, inner):
@@ -247,7 +266,8 @@
             return inner
 
         lax.fori_loop(0, CHUNK, come, 0)
-        physics(nth(i * CHUNK) // CHUNK, 1, upper, upper_sun[:, 0, :])
+        arrival(upper_sun.at[pl.ds(sun_row(i) * CHUNK, CHUNK)], upsun_recv.at[sun_row(i)]).wait()
+        physics(nth(i * CHUNK) // CHUNK, 1, upper, upper_sun)
 
         def one(j, inner):
             k = nth(i * CHUNK + j)
@@ -302,7 +322,7 @@
     arrival(sunlit.at[pl.ds(0, GROUPS - 1)], sun_send).wait()
     arrival(relay, leg1_send).wait()
     arrival(relay, leg2_send).wait()
-    up_sun.wait_send()
+    arrival(upper_sun, upsun_send).wait()
     arrival(relay, back1_send).wait()
     arrival(relay, back2_send).wait()
     arrival(outgoing.at[pl.ds(0, GROUPS - 1)], final_send).wait()
@@ -360,7 +380,7 @@
             half,
             pltpu.VMEM((SLOTS, 2 * HID), F32),
             dma((8,)),
-            dma((GROUPS,)), dma((2,)), dma((HALF,)), dma((HALF,)), dma, dma((HALF,)), dma((HALF,)), dma((GROUPS,)),
+            dma((GROUPS,)), dma((GROUPS // CHUNK,)), dma((HALF,)), dma((HALF,)), dma((HALF // CHUNK,)), dma((HALF,)), dma((HALF,)), dma((GROUPS,)),
             dma, dma, dma, dma, dma, dma, dma, dma,
         ],
         compiler_params=pltpu.CompilerParams(collective_id=0, has_side_effects=True),

time: 75.1 us -> 73.9 us (0.984)
  the two profiles are of different devices: /device:TPU:48 before, /device:TPU:112 now
where the time goes in v4:
time: 73.9 us; the launch traced here: 73.7 us
  Pallas kernels  73.1 us (99%)
    pallas_call x1, Pallas kernels, per_device(): pl.pallas_call(kernel, name='physics_remap', out_shape=(whole, pltpu.VMEM...  71.9 us

profile of v4, /device:TPU:112, one launch (start us, length us, event | category | flops | bytes accessed | tf_op | source)
XLA Modules:
  0.0 73.7 jit_solution(1943178101017404728)
XLA Ops:
  0.6 71.9 %physics_remap.1 = (bf16[32,32,256]{2,1,0:T(8,128)(2,1)S(1)}, bf16[512,1024]{1,0:T(8,128)(2,1)S(1)}, bf16[1024,512]{1,0:T(8,128)(2,1)S(1)}) custom-call(s32[1,512]{1,0:T(1,128)} %bitcast.2, s32[1,512]{1,0:T(1,128)} %bitcast.3, bf16[512,256]{1,0:T(8,128)(2,1)} %state_hbm.1, bf16[1024,512]{1,0:T(8,128)(2,1)} %cloud_hbm.1, bf16[768,256]{1,0:T(8,128)(2,1)} %cin_hbm.1, ...), custom_call_target="tpu_custom_call" | custom-call | tf_op jit(solution)/shard_map/physics_remap/pallas_call | solution.py:351
  72.6 1.2 %finish.1 = (bf16[512,256]{1,0:T(8,128)(2,1)}, bf16[1024,512]{1,0:T(8,128)(2,1)}) custom-call(bf16[512,1024]{1,0:T(8,128)(2,1)S(1)} %get-tuple-element.5.select, bf16[32,32,256]{2,1,0:T(8,128)(2,1)S(1)} %get-tuple-element.6.returned, bf16[1024,512]{1,0:T(8,128)(2,1)S(1)} %get-tuple-element.7.cloud), custom_call_target="tpu_custom_call" | custom-call | tf_op jit(solution)/shard_map/finish/pallas_call | solution.py:391

commit v5 on v4

--- a/solution.py
+++ b/solution.py
@@ -287,6 +287,14 @@
 
     lax.fori_loop(0, HALF, back2, 0)
 
+    def final(i, carry):
+        k = nth(i)
+        arrival(back_here.at[k], back2_recv.at[k]).wait()
+        hand_back(back_here.at[k], HALF + k)
+        return carry
+
+    lax.fori_loop(0, HALF, final, 0)
+
     def cloud_update(c, carry):
         rows = pl.ds(pl.multiple_of(c * ROWS, ROWS), ROWS)
         change = dot(second[rows, :], cout[:, 2 * LEV :])
@@ -304,14 +312,6 @@
         return carry
 
     lax.fori_loop(0, COLS // ROWS, selection, 0)
-
-    def final(i, carry):
-        k = nth(i)
-        arrival(back_here.at[k], back2_recv.at[k]).wait()
-        hand_back(back_here.at[k], HALF + k)
-        return carry
-
-    lax.fori_loop(0, HALF, final, 0)
 
     def final_arrival(k, carry):
         arrival(returned.at[k], final_recv.at[k]).wait()

time: 73.9 us -> 73.9 us (level)
  no operation moved by 1% of the time
where the time goes in v5:
time: 73.9 us; the launch traced here: 73.7 us
  Pallas kernels  73.1 us (99%)
    pallas_call x1, Pallas kernels, per_device(): pl.pallas_call(kernel, name='physics_remap', out_shape=(whole, pltpu.VMEM...  71.9 us

profile of v5, /device:TPU:112, one launch (start us, length us, event | category | flops | bytes accessed | tf_op | source)
XLA Modules:
  0.0 73.7 jit_solution(16520380604481445956)
XLA Ops:
  0.6 71.9 %physics_remap.1 = (bf16[32,32,256]{2,1,0:T(8,128)(2,1)S(1)}, bf16[512,1024]{1,0:T(8,128)(2,1)S(1)}, bf16[1024,512]{1,0:T(8,128)(2,1)S(1)}) custom-call(s32[1,512]{1,0:T(1,128)} %bitcast.2, s32[1,512]{1,0:T(1,128)} %bitcast.3, bf16[512,256]{1,0:T(8,128)(2,1)} %state_hbm.1, bf16[1024,512]{1,0:T(8,128)(2,1)} %cloud_hbm.1, bf16[768,256]{1,0:T(8,128)(2,1)} %cin_hbm.1, ...), custom_call_target="tpu_custom_call" | custom-call | tf_op jit(solution)/shard_map/physics_remap/pallas_call | solution.py:351
  72.6 1.2 %finish.1 = (bf16[512,256]{1,0:T(8,128)(2,1)}, bf16[1024,512]{1,0:T(8,128)(2,1)}) custom-call(bf16[512,1024]{1,0:T(8,128)(2,1)S(1)} %get-tuple-element.5.select, bf16[32,32,256]{2,1,0:T(8,128)(2,1)S(1)} %get-tuple-element.6.returned, bf16[1024,512]{1,0:T(8,128)(2,1)S(1)} %get-tuple-element.7.cloud), custom_call_target="tpu_custom_call" | custom-call | tf_op jit(solution)/shard_map/finish/pallas_call | solution.py:391
